TPU v7x, 32 devices: a whole 2x2x4 slice. The times are simulated.
32 devices in a mesh: spin: 2 (over core), band: 16 (over z, y, x).
Axes of the slice: x: 2, y: 2, z: 4, core: 2. Of those that a mesh axis runs over, the one named last changes fastest.
Arguments:
- orbitals: float32 [2, 16, 32768], P('spin', 'band'), may hold values from -15 to 15
- potential: float32 [32768], replicated, may hold values from -6 to 6
Outputs:
- updated: float32 [2, 16, 32768], P('spin', 'band')
- residual: float32 [2, 16, 32768], P('spin', 'band')
All inputs are finite; a program needn't handle non-finite values.
Results may differ from a plain program's by a relative error of at most 0.0003.
Values sent between devices are 32-bit elements; how exact they have to be, the bound alone decides.
A program may use at most 128 MiB of HBM per device.

v0:
```python
import math

import jax
import jax.numpy as jnp
from jax import lax
from jax.sharding import PartitionSpec as P

GRID = 32


screen_square = 0.04
hartree_weight = 0.03125
mixing = 0.25
step_length = 0.1


def passed_along(x, axis, by):
    peers = lax.axis_size(axis)
    return lax.ppermute(x, axis, [(i, (i + by) % peers) for i in range(peers)])


def cas_table(points):
    indices = jnp.arange(points, dtype=jnp.int32)
    phase_index = indices[:, None] * indices[None, :] % points
    angles = phase_index.astype(jnp.float32) * (2.0 * math.pi / points)
    return jnp.cos(angles) + jnp.sin(angles)


def wave_squares(points):
    indices = jnp.arange(points, dtype=jnp.int32)
    folded = jnp.where(indices < points // 2, indices, indices - points).astype(jnp.float32)
    wavenumber = folded * (math.pi / points)
    squares = wavenumber * wavenumber
    summed = squares[:, None, None] + squares[None, :, None] + squares[None, None, :]
    return summed.reshape(-1)


def plane_table(table):
    points = table.shape[0]
    joined = table[:, None, :, None] * table[None, :, None, :]
    return joined.reshape(points * points, points * points)


def hartley(signal, tables):
    table, joined = tables
    points = table.shape[0]
    leading = signal.shape[:-1]
    planes = signal.reshape((-1, points, points * points))
    planes = jnp.einsum("ka,sar->skr", table, planes, precision=lax.Precision.HIGHEST)
    planes = jnp.einsum("sar,qr->saq", planes, joined, precision=lax.Precision.HIGHEST)
    return planes.reshape(leading + (points**3,))


def screened(signal, tables, kernel):
    return hartley(kernel * hartley(signal, tables), tables) / kernel.shape[0]


def correlation(left_rows, right_rows):
    product = lax.dot_general(
        left_rows, right_rows, (((1,), (1,)), ((), ())), precision=lax.Precision.HIGHEST
    )
    return product / (left_rows.shape[1] * lax.axis_size("band"))


def remove(values, weights, basis):
    return values - lax.dot_general(
        weights, basis, (((0,), (0,)), ((), ())), precision=lax.Precision.HIGHEST
    )


def per_device(orbitals, potential):
    table = cas_table(GRID)
    tables = (table, plane_table(table))
    wave_square = wave_squares(GRID)
    kernel = jnp.where(wave_square > 0, 1.0 / (wave_square + screen_square), 0.0)
    volume = orbitals.shape[2]
    density = lax.psum(jnp.sum(orbitals * orbitals, axis=(0, 1)), ("spin", "band"))
    local_field = potential + hartree_weight * screened(density, tables, kernel)
    resident = orbitals[0]
    band_count = resident.shape[0]

    def pair_terms(left_rows, right_rows):
        pair_field = (left_rows[:, None, :] * right_rows[None, :, :]).reshape(-1, volume)
        return screened(pair_field, tables, kernel).reshape(band_count, band_count, volume)

    exchange_term = -jnp.sum(pair_terms(resident, resident) * resident[None, :, :], axis=1)
    for offset in (1, 2, -1, -2):
        partner = passed_along(resident, "band", offset)
        fields = pair_terms(resident, partner)
        exchange_term = exchange_term - jnp.sum(fields * partner[None, :, :], axis=1)
    kinetic = hartley(0.5 * wave_square * hartley(resident, tables), tables) / volume
    gradient = kinetic + local_field * resident + mixing * exchange_term
    orbital_slab, value_slab = (
        lax.all_to_all(resident, "band", split_axis=1, concat_axis=0, tiled=True),
        lax.all_to_all(gradient, "band", split_axis=1, concat_axis=0, tiled=True),
    )
    first_correlation, gram_matrix = lax.psum(
        (correlation(orbital_slab, value_slab), correlation(orbital_slab, orbital_slab)), "band"
    )
    second = first_correlation - jnp.dot(
        gram_matrix, first_correlation, precision=lax.Precision.HIGHEST
    )
    value_slab = remove(value_slab, first_correlation + second, orbital_slab)
    residual = lax.all_to_all(value_slab, "band", split_axis=0, concat_axis=1, tiled=True)
    return ((resident - step_length * residual)[None], residual[None])


def solution(mesh):
    return jax.shard_map(
        per_device,
        mesh=mesh,
        in_specs=(P("spin", "band", None), P()),
        out_specs=(P("spin", "band", None), P("spin", "band", None)),
        check_vma=False,
    )
```

profile of v0, /device:TPU:0, one launch (start us, length us, event | category | flops | bytes accessed | tf_op | source)
XLA Modules:
  0.0 300.6 jit_solution(5731318628276827684)
XLA Ops:
  7.2 6.1 %collective-permute-start.3 = (f32[1,32768]{1,0:T(1,128)}, f32[1,32768]{1,0:T(1,128)S(1)}, u32[]{:S(2)}, u32[]{:S(2)}) collective-permute-start(f32[1,32768]{1,0:T(1,128)} %bitcast.184), channel_id=1, source_target_pairs={{0,14},{1,15},{2,0},{3,1},{4,2},{5,3},{6,4},{7,5},{8,6},{9,7},{10,... | collective-permute-start | bytes 393224 | tf_op jit(solution)/shard_map/ppermute | solution.py:19
  16.2 7.0 %all-to-all-start.1 = ((f32[1,16,2048]{2,0,1:T(1,128)}), f32[1,16,2048]{2,0,1:T(1,128)S(1)}, u32[]{:S(2)}, u32[]{:S(2)}) async-start(f32[1,16,2048]{2,0,1:T(1,128)} %bitcast.188), calls=%async_computation.1 | async-start | bytes 262144 | tf_op jit(solution)/shard_map/all_to_all | solution.py:94
  23.3 8.0 %broadcast_multiply_fusion = f32[32,32,32,32]{3,2,1,0:T(8,128)} fusion(f32[32,32]{1,0:T(8,128)S(1)} %sine_add_fusion), kind=kLoop, calls=%fused_computation | loop fusion | flops 1048576 | bytes 4198400 | tf_op jit(solution)/shard_map/mul | solution.py:40
  31.3 13.7 %mul.632 = f32[1024,1024]{1,0:T(8,128)} reshape(f32[32,32,32,32]{3,2,1,0:T(8,128)} %broadcast_multiply_fusion) | data formatting | bytes 8388608 | tf_op jit(solution)/shard_map/mul | solution.py:40
  46.1 2.6 fusion.87
  50.3 6.2 %convolution_multiply_fusion.9 = f32[32,1024]{1,0:T(8,128)S(1)} fusion(f32[32,1024]{1,0:T(8,128)S(1)} %convolution_bitcast_fusion.9, f32[1024,1024]{1,0:T(8,128)} %mul.632, f32[32,1024]{1,0:T(8,128)S(1)} %add.355, f32[1024]{0:T(1024)S(1)} %add.356), kind=kOutput, calls=%fused_computation.16 | convolution fusion | flops 402849792 | bytes 4591616 | tf_op jit(solution)/shard_map/sar,qr->saq/dot_general | solution.py:50
  56.5 3.9 %convolution_multiply_fusion.1 = f32[32,1024]{1,0:T(8,128)S(1)} fusion(f32[32,1024]{1,0:T(8,128)S(1)} %convolution_bitcast_fusion.1, f32[1024,1024]{1,0:T(8,128)S(1)} %copy-done, f32[32,1024]{1,0:T(8,128)S(1)} %add.355, f32[1024]{0:T(1024)S(1)} %add.356), kind=kOutput, calls=%fused_computation.5 | convolution fusion | flops 402849792 | bytes 4591616 | tf_op jit(solution)/shard_map/sar,qr->saq/dot_general | solution.py:50
  60.8 3.9 %fusion.1 = f32[4,8,8,128]{3,2,1,0:T(8,128)S(1)} fusion(f32[32,1024]{1,0:T(8,128)S(1)} %convolution_bitcast_fusion, f32[1024,1024]{1,0:T(8,128)S(1)} %copy-done), kind=kOutput, calls=%fused_computation.4 | convolution fusion | flops 402685952 | bytes 4456448 | tf_op jit(solution)/shard_map/sar,qr->saq/dot_general | solution.py:50
  65.1 6.4 %convolution_multiply_fusion.3 = f32[32,1024]{1,0:T(8,128)S(1)} fusion(f32[32,1024]{1,0:T(8,128)S(1)} %convolution_bitcast_fusion.3, f32[1024,1024]{1,0:T(8,128)} %mul.632, f32[32,1024]{1,0:T(8,128)S(1)} %add.355, f32[1024]{0:T(1024)S(1)} %add.356), kind=kOutput, calls=%fused_computation.8 | convolution fusion | flops 402849792 | bytes 4591616 | tf_op jit(solution)/shard_map/sar,qr->saq/dot_general | solution.py:50
  71.8 3.9 %fusion.2 = f32[4,8,8,128]{3,2,1,0:T(8,128)S(1)} fusion(f32[32,1024]{1,0:T(8,128)S(1)} %convolution_bitcast_fusion.2, f32[1024,1024]{1,0:T(8,128)S(1)} %copy-done.1), kind=kOutput, calls=%fused_computation.7 | convolution fusion | flops 402685952 | bytes 4456448 | tf_op jit(solution)/shard_map/sar,qr->saq/dot_general | solution.py:50
  76.1 6.2 %convolution_multiply_fusion.5 = f32[32,1024]{1,0:T(8,128)S(1)} fusion(f32[32,1024]{1,0:T(8,128)S(1)} %convolution_bitcast_fusion.5, f32[1024,1024]{1,0:T(8,128)} %mul.632, f32[32,1024]{1,0:T(8,128)S(1)} %add.355, f32[1024]{0:T(1024)S(1)} %add.356), kind=kOutput, calls=%fused_computation.11 | convolution fusion | flops 402849792 | bytes 4591616 | tf_op jit(solution)/shard_map/sar,qr->saq/dot_general | solution.py:50
  82.7 3.9 %fusion.3 = f32[4,8,8,128]{3,2,1,0:T(8,128)S(1)} fusion(f32[32,1024]{1,0:T(8,128)S(1)} %convolution_bitcast_fusion.4, f32[1024,1024]{1,0:T(8,128)S(1)} %copy-done.2), kind=kOutput, calls=%fused_computation.10 | convolution fusion | flops 402685952 | bytes 4456448 | tf_op jit(solution)/shard_map/sar,qr->saq/dot_general | solution.py:50
  87.0 4.1 %convolution_multiply_fusion.8 = f32[32,1024]{1,0:T(8,128)S(1)} fusion(f32[32,1024]{1,0:T(8,128)S(1)} %convolution_bitcast_fusion.8, f32[1024,1024]{1,0:T(8,128)S(1)} %copy-done.2), kind=kOutput, calls=%fused_computation.15 | convolution fusion | flops 402685952 | bytes 4456448 | tf_op jit(solution)/shard_map/sar,qr->saq/dot_general | solution.py:50
  91.8 6.2 %convolution_multiply_fusion.7 = f32[32,1024]{1,0:T(8,128)S(1)} fusion(f32[32,1024]{1,0:T(8,128)S(1)} %convolution_bitcast_fusion.7, f32[1024,1024]{1,0:T(8,128)} %mul.632, f32[32,1024]{1,0:T(8,128)S(1)} %add.355, f32[1024]{0:T(1024)S(1)} %add.356), kind=kOutput, calls=%fused_computation.14 | convolution fusion | flops 402849792 | bytes 4591616 | tf_op jit(solution)/shard_map/sar,qr->saq/dot_general | solution.py:50
  98.4 3.9 %fusion.4 = f32[4,8,8,128]{3,2,1,0:T(8,128)S(1)} fusion(f32[32,1024]{1,0:T(8,128)S(1)} %convolution_bitcast_fusion.6, f32[1024,1024]{1,0:T(8,128)S(1)} %copy-done.3), kind=kOutput, calls=%fused_computation.13 | convolution fusion | flops 402685952 | bytes 4456448 | tf_op jit(solution)/shard_map/sar,qr->saq/dot_general | solution.py:50
  102.7 6.2 %convolution_multiply_fusion.13 = f32[32,1024]{1,0:T(8,128)S(1)} fusion(f32[32,1024]{1,0:T(8,128)S(1)} %fusion.27, f32[1024,1024]{1,0:T(8,128)} %mul.632, f32[32,1024]{1,0:T(8,128)S(1)} %add.355, f32[1024]{0:T(1024)S(1)} %add.356), kind=kOutput, calls=%fused_computation.22 | convolution fusion | flops 402751488 | bytes 4591616 | tf_op jit(solution)/shard_map/sar,qr->saq/dot_general | solution.py:50
  109.3 4.1 %fusion.6 = f32[4,8,8,128]{3,2,1,0:T(8,128)S(1)} fusion(f32[32,1024]{1,0:T(8,128)S(1)} %convolution_bitcast_fusion.12, f32[1024,1024]{1,0:T(8,128)S(1)} %copy-done.4), kind=kOutput, calls=%fused_computation.21 | convolution fusion | flops 402685952 | bytes 4456448 | tf_op jit(solution)/shard_map/sar,qr->saq/dot_general | solution.py:50
  113.6 68.9 %all-reduce.3.cloned.1.call-done = f32[32,1024]{1,0:T(8,128)} async-done(((f32[32,1024]{1,0:T(8,128)}), f32[32,1024]{1,0:T(8,128)}) %all-reduce.3.cloned.1.call-update) | async-done | bytes 131088 | tf_op jit(solution)/shard_map/psum | solution.py:77
  183.9 6.1 %convolution_multiply_fusion.11 = f32[32,1024]{1,0:T(8,128)S(1)} fusion(f32[32,1024]{1,0:T(8,128)S(1)} %convolution_bitcast_fusion.11, f32[1024,1024]{1,0:T(8,128)} %mul.632, f32[32,1024]{1,0:T(8,128)S(1)} %add.355, f32[1024]{0:T(1024)S(1)} %add.356), kind=kOutput, calls=%fused_computation.19 | convolution fusion | flops 402849792 | bytes 4591616 | tf_op jit(solution)/shard_map/sar,qr->saq/dot_general | solution.py:50
  190.3 3.9 %fusion.5 = f32[4,8,8,128]{3,2,1,0:T(8,128)S(1)} fusion(f32[32,1024]{1,0:T(8,128)S(1)} %convolution_bitcast_fusion.10, f32[1024,1024]{1,0:T(8,128)S(1)} %copy-done.5), kind=kOutput, calls=%fused_computation.18 | convolution fusion | flops 402685952 | bytes 4456448 | tf_op jit(solution)/shard_map/sar,qr->saq/dot_general | solution.py:50
  195.0 4.7 %all-to-all-start = ((f32[1,16,2048]{2,0,1:T(1,128)}), f32[1,16,2048]{2,0,1:T(1,128)S(1)}, u32[]{:S(2)}, u32[]{:S(2)}) async-start(f32[1,16,2048]{2,0,1:T(1,128)} %bitcast.50), calls=%async_computation | async-start | bytes 262144 | tf_op jit(solution)/shard_map/all_to_all | solution.py:95
  199.9 7.6 %all-to-all-done = f32[1,16,2048]{2,0,1:T(1,128)S(1)} async-done(((f32[1,16,2048]{2,0,1:T(1,128)}), f32[1,16,2048]{2,0,1:T(1,128)S(1)}, u32[]{:S(2)}, u32[]{:S(2)}) %all-to-all-start) | async-done | bytes 131104 | tf_op jit(solution)/shard_map/all_to_all | solution.py:95
  207.8 73.1 %all-reduce = (f32[16,16]{0,1:T(8,128)S(1)}, f32[16,16]{1,0:T(8,128)S(1)}) all-reduce(f32[16,16]{0,1:T(8,128)S(1)} %fusion.8, f32[16,16]{1,0:T(8,128)S(1)} %convolution_multiply_fusion.14), channel_id=1, replica_groups=mesh['spin'=2,'band'=16] {'band'}, use_global_device_ids=true, to_apply=%region_1.2 | all-reduce | flops 512 | bytes 4096 | tf_op jit(solution)/shard_map/psum | solution.py:97
  281.5 10.4 %all_to_all.48 = f32[16,1,2048]{2,1,0:T(1,128)S(1)} all-to-all(f32[16,1,2048]{2,1,0:T(1,128)S(1)} %copy.4), channel_id=1, replica_groups=mesh['spin'=2,'band'=16] {'band'}, dimensions={0} | all-to-all | bytes 262144 | tf_op jit(solution)/shard_map/all_to_all | solution.py:104
  (72 shorter events, 14.9 us)
Async XLA Ops:
  7.2 38.4 %collective-permute-start.3 = (f32[1,32768]{1,0:T(1,128)}, f32[1,32768]{1,0:T(1,128)S(1)}, u32[]{:S(2)}, u32[]{:S(2)}) collective-permute-start(f32[1,32768]{1,0:T(1,128)} %bitcast.184), channel_id=1, source_target_pairs={{0,14},{1,15},{2,0},{3,1},{4,2},{5,3},{6,4},{7,5},{8,6},{9,7},{10,... | collective-permute-start | bytes 393224 | tf_op jit(solution)/shard_map/ppermute | solution.py:19
  13.2 32.4 %collective-permute-start.2 = (f32[1,32768]{1,0:T(1,128)}, f32[1,32768]{1,0:T(1,128)S(1)}, u32[]{:S(2)}, u32[]{:S(2)}) collective-permute-start(f32[1,32768]{1,0:T(1,128)} %bitcast.185), channel_id=1, source_target_pairs={{0,15},{1,0},{2,1},{3,2},{4,3},{5,4},{6,5},{7,6},{8,7},{9,8},{10,9... | collective-permute-start | bytes 393224 | tf_op jit(solution)/shard_map/ppermute | solution.py:19
  14.7 30.9 %collective-permute-start.1 = (f32[1,32768]{1,0:T(1,128)}, f32[1,32768]{1,0:T(1,128)S(1)}, u32[]{:S(2)}, u32[]{:S(2)}) collective-permute-start(f32[1,32768]{1,0:T(1,128)} %bitcast.186), channel_id=1, source_target_pairs={{0,2},{1,3},{2,4},{3,5},{4,6},{5,7},{6,8},{7,9},{8,10},{9,11},{10,... | collective-permute-start | bytes 393224 | tf_op jit(solution)/shard_map/ppermute | solution.py:19
  16.2 29.4 %collective-permute-start = (f32[1,32768]{1,0:T(1,128)}, f32[1,32768]{1,0:T(1,128)S(1)}, u32[]{:S(2)}, u32[]{:S(2)}) collective-permute-start(f32[1,32768]{1,0:T(1,128)} %bitcast.187), channel_id=1, source_target_pairs={{0,1},{1,2},{2,3},{3,4},{4,5},{5,6},{6,7},{7,8},{8,9},{9,10},{10,1... | collective-permute-start | bytes 393224 | tf_op jit(solution)/shard_map/ppermute | solution.py:19
  16.2 178.8 %all-to-all-start.1 = ((f32[1,16,2048]{2,0,1:T(1,128)}), f32[1,16,2048]{2,0,1:T(1,128)S(1)}, u32[]{:S(2)}, u32[]{:S(2)}) async-start(f32[1,16,2048]{2,0,1:T(1,128)} %bitcast.188), calls=%async_computation.1 | async-start | bytes 262144 | tf_op jit(solution)/shard_map/all_to_all | solution.py:94
  31.3 14.9 %copy-start.6 = (f32[1,1,32768]{2,1,0:T(1,128)S(1)}, f32[1,1,32768]{2,1,0:T(1,128)}, u32[]{:S(2)}) copy-start(f32[1,1,32768]{2,1,0:T(1,128)} %param.2) | copy-start | bytes 393220
  49.2 0.9 copy-start.7
  49.6 132.9 %all-reduce.3.cloned.1.call-start = ((), (), s32[]{:S(2)}) async-start(), calls=%async_computation.3 | async-start | bytes 262144 | tf_op jit(solution)/shard_map/psum | solution.py:77
  50.3 6.2 %copy-start = (f32[1024,1024]{1,0:T(8,128)S(1)}, f32[1024,1024]{1,0:T(8,128)}, u32[]{:S(2)}) copy-start(f32[1024,1024]{1,0:T(8,128)} %mul.632) | copy-start | bytes 12582916
  64.7 7.1 %copy-start.1 = (f32[1024,1024]{1,0:T(8,128)S(1)}, f32[1024,1024]{1,0:T(8,128)}, u32[]{:S(2)}) copy-start(f32[1024,1024]{1,0:T(8,128)} %mul.632) | copy-start | bytes 12582916
  75.7 7.0 %copy-start.2 = (f32[1024,1024]{1,0:T(8,128)S(1)}, f32[1024,1024]{1,0:T(8,128)}, u32[]{:S(2)}) copy-start(f32[1024,1024]{1,0:T(8,128)} %mul.632) | copy-start | bytes 12582916
  91.4 6.9 %copy-start.3 = (f32[1024,1024]{1,0:T(8,128)S(1)}, f32[1024,1024]{1,0:T(8,128)}, u32[]{:S(2)}) copy-start(f32[1024,1024]{1,0:T(8,128)} %mul.632) | copy-start | bytes 12582916
  102.3 7.0 %copy-start.4 = (f32[1024,1024]{1,0:T(8,128)S(1)}, f32[1024,1024]{1,0:T(8,128)}, u32[]{:S(2)}) copy-start(f32[1024,1024]{1,0:T(8,128)} %mul.632) | copy-start | bytes 12582916
  182.5 7.8 %copy-start.5 = (f32[1024,1024]{1,0:T(8,128)S(1)}, f32[1024,1024]{1,0:T(8,128)}, u32[]{:S(2)}) copy-start(f32[1024,1024]{1,0:T(8,128)} %mul.632) | copy-start | bytes 12582916
  183.9 10.4 %copy-start.8 = (f32[32768]{0:T(1024)S(1)}, f32[32768]{0:T(1024)}, u32[]{:S(2)}) copy-start(f32[32768]{0:T(1024)} %param.3) | copy-start | bytes 393220
  195.0 12.5 %all-to-all-start = ((f32[1,16,2048]{2,0,1:T(1,128)}), f32[1,16,2048]{2,0,1:T(1,128)S(1)}, u32[]{:S(2)}, u32[]{:S(2)}) async-start(f32[1,16,2048]{2,0,1:T(1,128)} %bitcast.50), calls=%async_computation | async-start | bytes 262144 | tf_op jit(solution)/shard_map/all_to_all | solution.py:95
Sparse Core Ops, SparseCore 0:
  56.5 125.9 all-reduce.2
where the time goes:
time: 306 us; the launch traced here: 301 us
  blocking collectives  83.5 us (27%)
  waiting for transfers between devices  76.7 us (25%)
  matrix products  75.7 us (25%)
  starting transfers between devices  21.2 us (7%)
  local copies, waits for them, and re-layouts  16 us (5%)
  between operations  15 us (5%)
  other arithmetic  12.5 us (4%)
    psum x1, blocking collectives, per_device(): lax.psum((correlation(orbital_slab, value_slab), correlation(orbital_slab...  73.1 us
    psum x1, waiting for transfers between devices, per_device(): lax.psum(jnp.sum(orbitals * orbitals, axis=(0, 1)), ('spin', 'band'))  68.9 us
    dot_general x14, matrix products, hartley(): jnp.einsum('sar,qr->saq', planes, joined, precision=lax.Precision.HIGHEST)  68.8 us
    mul x1, local copies, waits for them, and re-layouts, plane_table(): joined = table[:, None, :, None] * table[None, :, None, :]  13.7 us
    all_to_all x1, blocking collectives, per_device(): lax.all_to_all(value_slab, 'band', split_axis=0, concat_axis=1, tiled=True)  10.4 us
    ppermute x4, starting transfers between devices, passed_along(): return lax.ppermute(x, axis, [(i, (i + by) % peers) for i in range(peers)])  9.04 us
    mul x1, other arithmetic, plane_table(): joined = table[:, None, :, None] * table[None, :, None, :]  7.97 us
    all_to_all x1, waiting for transfers between devices, per_device(): lax.all_to_all(gradient, 'band', split_axis=1, concat_axis=0, tiled=True)  7.55 us
  transfers between devices with their start and end apart: 7, of which 2 were waited for; matrix products, arithmetic and copies ran while one was open for 34% of the time, Pallas kernels for 0%

commit v1 on v0

v1 whole, which is shorter than its diff:
```python
import functools
import math

import jax
import jax.numpy as jnp
import numpy as np
from jax import lax
from jax.experimental import pallas as pl
from jax.experimental.pallas import tpu as pltpu
from jax.sharding import PartitionSpec as P

screen_square = 0.04
hartree_weight = 0.03125
mixing = 0.25
step_length = 0.1

MESH = pl.DeviceIdType.MESH
LANES = 128


def line_sizes(count):
    power = int(math.log2(count)) if count > 1 else 0
    if 2**power != count:
        return (count, 1, 1)
    fast = 2 ** (power // 3)
    return (count // (fast * fast), fast, fast)


def offsets_of(size):
    if size == 1:
        return (0,)
    if size == 2:
        return (0, 1)
    return tuple(range(-(size - 1), size))


def bf16_split(x):
    high = x.astype(jnp.bfloat16)
    return high, (x - high.astype(jnp.float32)).astype(jnp.bfloat16)


def dot(a, b):
    return jnp.dot(a, b, preferred_element_type=jnp.float32)


class Gather:
    def __init__(self, count, sizes, own, slots, send_sem, recv_sem):
        self.count, self.sizes, self.own, self.slots = count, sizes, own, slots
        self.send_sem, self.recv_sem = send_sem, recv_sem
        self.rows = own.shape[0] // 2
        self.me = lax.axis_index("band")
        self.spin = lax.axis_index("spin")
        strides = (sizes[1] * sizes[2], sizes[2], 1)
        self.strides = strides
        self.coords = tuple(lax.rem(self.me // strides[d], sizes[d]) for d in range(3))
        self.sent = []

    def neighbours(self):
        found = []
        for d in range(3):
            for way in self.ways(d):
                found.append(self.neighbour(d, way))
        return found

    def ways(self, d):
        return () if self.sizes[d] == 1 else (1,) if self.sizes[d] == 2 else (1, -1)

    def neighbour(self, d, way):
        c = self.coords[d]
        if self.sizes[d] == 2:
            return None, self.me + (1 - 2 * c) * self.strides[d]
        guard = c + way < self.sizes[d] if way > 0 else c + way >= 0
        return guard, self.me + way * self.strides[d]

    def part(self, half):
        return pl.ds(half * self.rows, self.rows)

    def send(self, half, block, d, way, guard, mine):
        ok, target = self.neighbour(d, way)
        for extra in (guard,):
            if extra is not None:
                ok = extra if ok is None else jnp.logical_and(ok, extra)
        source = self.own.at[self.part(half)] if mine else self.slots.at[block, self.part(half)]
        copy = pltpu.make_async_remote_copy(
            src_ref=source,
            dst_ref=self.slots.at[block, self.part(half)],
            send_sem=self.send_sem.at[len(self.sent)],
            recv_sem=self.recv_sem.at[half, block],
            device_id=(self.spin, target),
            device_id_type=MESH,
        )
        self.sent.append((ok, copy))
        if ok is None:
            copy.start()
        else:
            pl.when(ok)(copy.start)

    def order(self, half):
        return (0, 1, 2) if half == 0 else (0, 2, 1)

    def send_own(self):
        for half in range(2):
            for d in self.order(half):
                for way in self.ways(d):
                    self.send(half, self.me, d, way, None, True)

    def events(self):
        found = []
        for half in range(2):
            for z in offsets_of(self.sizes[0]):
                for y in offsets_of(self.sizes[1]):
                    for x in offsets_of(self.sizes[2]):
                        if (z, y, x) != (0, 0, 0):
                            found.append((abs(z) + abs(y) + abs(x), half, (z, y, x)))
        return sorted(found, key=lambda e: (e[0], -abs(e[2][0]), e[1]))

    def take(self, half, offsets):
        guard, block = None, self.me
        for d, o in enumerate(offsets):
            if o == 0:
                continue
            c = self.coords[d]
            if self.sizes[d] == 2:
                block = block + (1 - 2 * c) * self.strides[d]
            else:
                ok = c + o < self.sizes[d] if o > 0 else c + o >= 0
                guard = ok if guard is None else jnp.logical_and(guard, ok)
                block = block + o * self.strides[d]
        if guard is not None:
            block = jnp.where(guard, block, self.me)
        arrived = self.slots.at[block, self.part(half)]
        wait = pltpu.make_async_remote_copy(
            src_ref=arrived,
            dst_ref=arrived,
            send_sem=self.send_sem.at[0],
            recv_sem=self.recv_sem.at[half, block],
            device_id=(self.spin, self.me),
            device_id_type=MESH,
        ).wait_recv
        if guard is None:
            wait()
        else:
            pl.when(guard)(wait)
        order = self.order(half)
        last = max(p for p in range(3) if offsets[order[p]] != 0)
        d = order[last]
        if self.sizes[d] > 2:
            self.send(half, block, d, -1 if offsets[d] > 0 else 1, guard, False)
        for later in order[last + 1 :]:
            for way in self.ways(later):
                self.send(half, block, later, way, guard, False)

    def finish(self):
        for ok, copy in self.sent:
            if ok is None:
                copy.wait_send()
            else:
                pl.when(ok)(copy.wait_send)


class DirectGather:
    def __init__(self, count, own, slots, send_sem, recv_sem):
        self.count, self.own, self.slots = count, own, slots
        self.send_sem, self.recv_sem = send_sem, recv_sem
        self.me = lax.axis_index("band")
        self.spin = lax.axis_index("spin")

    def copy(self, block, target):
        return pltpu.make_async_remote_copy(
            src_ref=self.own,
            dst_ref=self.slots.at[block],
            send_sem=self.send_sem.at[target],
            recv_sem=self.recv_sem.at[0, block],
            device_id=(self.spin, target),
            device_id_type=MESH,
        )

    def each(self, action):
        def step(k, carry):
            action(lax.rem(self.me + k, self.count))
            return carry

        lax.fori_loop(1, self.count, step, 0)

    def send_own(self):
        self.each(lambda other: self.copy(self.me, other).start())

    def take_all(self):
        self.each(lambda other: self.copy(other, other).wait_recv())

    def finish(self):
        self.each(lambda other: self.copy(self.me, other).wait_send())


def relayed(count, sizes):
    return math.prod(len(offsets_of(s)) for s in sizes) <= 64 and count > 1


def kernel(
    count, spins, points,
    own, potential, row_factor, column_factor, left_high, left_low, green, wave,
    updated, residual,
    slots, table_high, table_low, density, other_density, cube, flat,
    send_sem, recv_sem, swap_sem,
):
    volume = points**3
    plane = points * points
    blocks = plane // LANES
    sizes = line_sizes(count)
    me = lax.axis_index("band")
    spin = lax.axis_index("spin")
    relay = relayed(count, sizes)

    barrier = pltpu.get_barrier_semaphore()
    expected = jnp.int32(0)
    if relay:
        gather = Gather(count, sizes, own, slots, send_sem, recv_sem)
        for ok, target in gather.neighbours():
            def greet(target=target):
                pl.semaphore_signal(barrier, inc=1, device_id=(spin, target), device_id_type=MESH)

            if ok is None:
                greet()
                expected = expected + 1
            else:
                pl.when(ok)(greet)
                expected = expected + ok.astype(jnp.int32)
    else:
        gather = DirectGather(count, own, slots, send_sem, recv_sem)
        gather.each(
            lambda other: pl.semaphore_signal(barrier, inc=1, device_id=(spin, other), device_id_type=MESH)
        )
        expected = expected + (count - 1)
    for away in range(1, spins):
        pl.semaphore_signal(
            barrier, inc=1, device_id=(lax.rem(spin + away, spins), me), device_id_type=MESH
        )
    pl.semaphore_wait(barrier, expected + (spins - 1))
    gather.send_own()

    def build(y, carry):
        rows = pl.ds(pl.multiple_of(y * points, points), points)
        high, low = bf16_split(row_factor[pl.ds(y, 1), :] * column_factor[...])
        table_high[rows, :] = high
        table_low[rows, :] = low
        return carry

    lax.fori_loop(0, points, build, 0)

    def as_cube(ref):
        return jnp.concatenate(
            [ref[pl.ds(k, points, stride=blocks), :] for k in range(blocks)], axis=1
        )

    def transform(fields):
        rows = fields.shape[0]
        high, low = bf16_split(fields)
        lh, ll = left_high[:rows, :rows], left_low[:rows, :rows]
        turned = dot(lh, high) + dot(lh, low) + dot(ll, high)
        high, low = bf16_split(turned)
        both = dot(jnp.concatenate([high, low], axis=0), table_high[...])
        return both[:rows] + both[rows:] + dot(high, table_low[...])

    def scaled(fields, factors):
        return jnp.concatenate(
            [fields[k * points : (k + 1) * points] * f for k, f in enumerate(factors)], axis=0
        )

    resident = as_cube(own)
    slots[me] = own[...]
    first = transform(jnp.concatenate([resident, resident * resident], axis=0))
    first = transform(scaled(first, (wave[...], green[...])))
    cube[...] = first[:points] - mixing * (first[points:] * resident)

    if relay:
        for _, half, offsets in gather.events():
            gather.take(half, offsets)
    else:
        gather.take_all()

    def add_square(j, total):
        band = slots[j]
        return total + band * band

    density[...] = lax.fori_loop(0, count, add_square, jnp.zeros(own.shape, jnp.float32))
    swaps = []
    for away in range(1, spins):
        swap = pltpu.make_async_remote_copy(
            src_ref=density,
            dst_ref=other_density.at[away - 1],
            send_sem=swap_sem.at[0, away - 1],
            recv_sem=swap_sem.at[1, away - 1],
            device_id=(lax.rem(spin + away, spins), me),
            device_id_type=MESH,
        )
        swap.start()
        swaps.append(swap)

    partners = [as_cube(slots.at[lax.rem(me + o + count, count)]) for o in (1, 2, -1, -2)]
    fields = transform(jnp.concatenate([resident * p for p in partners], axis=0))
    fields = transform(scaled(fields, (green[...],) * len(partners)))
    exchange = cube[...]
    for k, p in enumerate(partners):
        exchange = exchange - mixing * (fields[k * points : (k + 1) * points] * p)

    for swap in swaps:
        swap.wait()
    total = as_cube(density)
    for away in range(1, spins):
        total = total + as_cube(other_density.at[away - 1])
    screened = transform(transform(total) * green[...])
    local = as_cube(potential) + hartree_weight * screened
    gradient = exchange + local * resident
    for k in range(blocks):
        flat[pl.ds(k, points, stride=blocks), :] = gradient[:, k * LANES : (k + 1) * LANES]

    def project(values):
        def step(j, left):
            band = slots[j]
            share = jnp.sum(jnp.sum(band * values, axis=0, keepdims=True), axis=1, keepdims=True)
            return left - (share / volume) * band

        return lax.fori_loop(0, count, step, values)

    flat[...] = project(flat[...])
    result = project(flat[...])
    residual[...] = result
    updated[...] = own[...] - step_length * result
    gather.finish()


def tables(points, batch):
    indices = np.arange(points)
    angles = (indices[:, None] * indices[None, :] % points) * (2.0 * math.pi / points)
    table = (np.cos(angles) + np.sin(angles)).astype(np.float32)
    left = np.kron(np.eye(batch, dtype=np.float32), table)
    folded = np.where(indices < points // 2, indices, indices - points) * (math.pi / points)
    square = folded * folded
    summed = square[:, None, None] + square[None, :, None] + square[None, None, :]
    summed = summed.reshape(points, points * points)
    volume = points**3
    green = np.where(summed > 0, 1.0 / (summed + screen_square), 0.0) / volume
    wave = 0.5 * summed / volume
    return (
        np.repeat(table, points, axis=1),
        np.tile(table, (1, points)),
        left,
        green.astype(np.float32),
        wave.astype(np.float32),
    )


def per_device(count, spins, orbitals, potential):
    volume = orbitals.shape[2]
    points = round(volume ** (1 / 3))
    rows = volume // LANES
    row_factor, column_factor, left, green, wave = tables(points, 4)
    left_high = left.astype(jnp.bfloat16)
    left_low = (left - left_high.astype(np.float32)).astype(jnp.bfloat16)
    sizes = line_sizes(count)
    if relayed(count, sizes):
        sends = 12 + 4 * 2 * math.prod(len(offsets_of(s)) for s in sizes)
    else:
        sends = count
    vmem = pl.BlockSpec(memory_space=pltpu.VMEM)
    flat_shape = jax.ShapeDtypeStruct((rows, LANES), jnp.float32)
    updated, residual = pl.pallas_call(
        functools.partial(kernel, count, spins, points),
        out_shape=(flat_shape, flat_shape),
        in_specs=[vmem] * 8,
        out_specs=(vmem, vmem),
        scratch_shapes=[
            pltpu.VMEM((count, rows, LANES), jnp.float32),
            pltpu.VMEM((points * points, points * points), jnp.bfloat16),
            pltpu.VMEM((points * points, points * points), jnp.bfloat16),
            pltpu.VMEM((rows, LANES), jnp.float32),
            pltpu.VMEM((max(spins - 1, 1), rows, LANES), jnp.float32),
            pltpu.VMEM((points, points * points), jnp.float32),
            pltpu.VMEM((rows, LANES), jnp.float32),
            pltpu.SemaphoreType.DMA((sends,)),
            pltpu.SemaphoreType.DMA((2, count)),
            pltpu.SemaphoreType.DMA((2, max(spins - 1, 1))),
        ],
        compiler_params=pltpu.CompilerParams(
            collective_id=0, has_side_effects=True, vmem_limit_bytes=60 * 1024 * 1024
        ),
    )(
        orbitals.reshape(rows, LANES), potential.reshape(rows, LANES),
        row_factor, column_factor, left_high, left_low, green, wave,
    )
    return updated.reshape(orbitals.shape), residual.reshape(orbitals.shape)


def solution(mesh):
    return jax.shard_map(
        functools.partial(per_device, mesh.shape["band"], mesh.shape["spin"]),
        mesh=mesh,
        in_specs=(P("spin", "band", None), P()),
        out_specs=(P("spin", "band", None), P("spin", "band", None)),
        check_vma=False,
    )
```

time: 306 us -> 41.5 us (0.14); the launches traced: 301 us -> 41.4 us
  blocking collectives: 83.5 us -> 0 us
  waiting for transfers between devices: 76.7 us -> 0 us
  matrix products: 75.7 us -> 0 us
  Pallas kernels: 0 us -> 38.4 us
  starting transfers between devices: 21.2 us -> 0 us
  between operations: 15 us -> 0.65 us
  local copies, waits for them, and re-layouts: 16 us -> 2.26 us
  other arithmetic: 12.5 us -> 0 us
    dot_general x32 -> x0, matrix products: 75.7 us -> none  [the longest x14 68.8 us: hartley(): jnp.einsum('sar,qr->saq', planes, joined, precision=lax.Precision.HIGHEST)]
    psum x1 -> x0, blocking collectives: 73.1 us -> none  [per_device(): lax.psum((correlation(orbital_slab, value_slab), correlation(orbital_slab...]
    psum x1 -> x0, waiting for transfers between devices: 68.9 us -> none  [per_device(): lax.psum(jnp.sum(orbitals * orbitals, axis=(0, 1)), ('spin', 'band'))]
    pallas_call x0 -> x1, Pallas kernels: none -> 38.4 us  [per_device(): pl.pallas_call(functools.partial(kernel, count, spins, points), out_shape...]
    mul x1 -> x0, local copies, waits for them, and re-layouts: 13.7 us -> none  [plane_table(): joined = table[:, None, :, None] * table[None, :, None, :]]
    all_to_all x2 -> x0, starting transfers between devices: 11.7 us -> none  [the longest x1 7 us: per_device(): lax.all_to_all(resident, 'band', split_axis=1, concat_axis=0, tiled=True)]
    all_to_all x1 -> x0, blocking collectives: 10.4 us -> none  [per_device(): lax.all_to_all(value_slab, 'band', split_axis=0, concat_axis=1, tiled=True)]
    ppermute x4 -> x0, starting transfers between devices: 9.04 us -> none  [passed_along(): return lax.ppermute(x, axis, [(i, (i + by) % peers) for i in range(peers)])]
  transfers between devices with their start and end apart: 7 -> 0, of which waited for: 2 -> 0; matrix products, arithmetic and copies ran while one was open for 34% -> 0% of each run, Pallas kernels for 0% -> 0%
where the time goes in v1:
time: 41.5 us; the launch traced here: 41.4 us
  Pallas kernels  38.4 us (93%)
  local copies, waits for them, and re-layouts  2.26 us (5%)
  between operations  0.65 us (2%)
    pallas_call x1, Pallas kernels, per_device(): pl.pallas_call(functools.partial(kernel, count, spins, points), out_shape...  38.4 us
    unnamed x4, local copies, waits for them, and re-layouts  2.26 us

profile of v1, /device:TPU:0, one launch (start us, length us, event | category | flops | bytes accessed | tf_op | source)
XLA Modules:
  0.0 41.4 jit_solution(7512594368828950280)
XLA Ops:
  0.6 38.4 %shard_map.95 = (f32[256,128]{1,0:T(8,128)}, f32[256,128]{1,0:T(8,128)}) custom-call(f32[256,128]{1,0:T(8,128)} %bitcast.6, f32[256,128]{1,0:T(8,128)} %bitcast.7, f32[32,1024]{1,0:T(8,128)} %constant.12.clone.row_factor, f32[32,1024]{1,0:T(8,128)} %constant.13.clone.column_factor, bf16[128,128]{1,0:T(8,128)(2,1)} %constant.14.clone.left_high, ...), custom_call_target="tpu_custom_call" | custom-call | tf_op jit(solution)/shard_map/pallas_call | solution.py:367
  39.1 0.0 copy-start
  39.1 1.6 %copy.12 = f32[1,1,32768]{2,1,0:T(1,128)} copy(f32[1,1,32768]{2,1,0:T(1,128)} %bitcast.5) | data formatting | bytes 262144
  40.7 0.0 copy-done
  40.7 0.7 %copy.13 = f32[1,1,32768]{2,1,0:T(1,128)} copy(f32[1,1,32768]{2,1,0:T(1,128)S(1)} %bitcast.4) | data formatting | bytes 262144
Async XLA Ops:
  39.1 1.6 %copy-start = (f32[256,128]{1,0:T(8,128)S(1)}, f32[256,128]{1,0:T(8,128)}, u32[]{:S(2)}) copy-start(f32[256,128]{1,0:T(8,128)} %get-tuple-element.5) | copy-start | bytes 393220

commit v2 on v1

--- a/solution.py
+++ b/solution.py
@@ -16,6 +16,8 @@
 
 MESH = pl.DeviceIdType.MESH
 LANES = 128
+PARTS = (((0, 1, 2), 16), ((0, 2, 1), 16))
+PART_UNITS = sum(share for _, share in PARTS)
 
 
 def line_sizes(count):
@@ -47,7 +49,12 @@
     def __init__(self, count, sizes, own, slots, send_sem, recv_sem):
         self.count, self.sizes, self.own, self.slots = count, sizes, own, slots
         self.send_sem, self.recv_sem = send_sem, recv_sem
-        self.rows = own.shape[0] // 2
+        rows = own.shape[0]
+        bounds = [0]
+        for _, share in PARTS:
+            bounds.append(bounds[-1] + rows * share // PART_UNITS)
+        bounds[-1] = rows
+        self.bounds = bounds
         self.me = lax.axis_index("band")
         self.spin = lax.axis_index("spin")
         strides = (sizes[1] * sizes[2], sizes[2], 1)
@@ -73,16 +80,14 @@
         return guard, self.me + way * self.strides[d]
 
     def part(self, half):
-        return pl.ds(half * self.rows, self.rows)
-
-    def send(self, half, block, d, way, guard, mine):
+        return pl.ds(self.bounds[half], self.bounds[half + 1] - self.bounds[half])
+
+    def send(self, half, block, d, way, guard):
         ok, target = self.neighbour(d, way)
-        for extra in (guard,):
-            if extra is not None:
-                ok = extra if ok is None else jnp.logical_and(ok, extra)
-        source = self.own.at[self.part(half)] if mine else self.slots.at[block, self.part(half)]
+        if guard is not None:
+            ok = guard if ok is None else jnp.logical_and(ok, guard)
         copy = pltpu.make_async_remote_copy(
-            src_ref=source,
+            src_ref=self.slots.at[block, self.part(half)],
             dst_ref=self.slots.at[block, self.part(half)],
             send_sem=self.send_sem.at[len(self.sent)],
             recv_sem=self.recv_sem.at[half, block],
@@ -96,23 +101,31 @@
             pl.when(ok)(copy.start)
 
     def order(self, half):
-        return (0, 1, 2) if half == 0 else (0, 2, 1)
+        return PARTS[half][0]
 
     def send_own(self):
-        for half in range(2):
-            for d in self.order(half):
+        for step in range(3):
+            for half in reversed(range(len(PARTS))):
+                d = self.order(half)[step]
                 for way in self.ways(d):
-                    self.send(half, self.me, d, way, None, True)
+                    self.send(half, self.me, d, way, None)
 
     def events(self):
         found = []
-        for half in range(2):
+        for half in range(len(PARTS)):
             for z in offsets_of(self.sizes[0]):
                 for y in offsets_of(self.sizes[1]):
                     for x in offsets_of(self.sizes[2]):
                         if (z, y, x) != (0, 0, 0):
                             found.append((abs(z) + abs(y) + abs(x), half, (z, y, x)))
-        return sorted(found, key=lambda e: (e[0], -abs(e[2][0]), e[1]))
+        found = sorted(found, key=lambda e: (e[0], -e[1], -abs(e[2][0])))
+        onward = [e[1:] for e in found if not self.ends(*e[1:])]
+        return onward, [e[1:] for e in found if self.ends(*e[1:])]
+
+    def ends(self, half, offsets):
+        d = self.order(half)[2]
+        o = offsets[d]
+        return o != 0 and (self.sizes[d] <= 2 or abs(o) == self.sizes[d] - 1)
 
     def take(self, half, offsets):
         guard, block = None, self.me
@@ -145,10 +158,10 @@
         last = max(p for p in range(3) if offsets[order[p]] != 0)
         d = order[last]
         if self.sizes[d] > 2:
-            self.send(half, block, d, -1 if offsets[d] > 0 else 1, guard, False)
+            self.send(half, block, d, -1 if offsets[d] > 0 else 1, guard)
         for later in order[last + 1 :]:
             for way in self.ways(later):
-                self.send(half, block, later, way, guard, False)
+                self.send(half, block, later, way, guard)
 
     def finish(self):
         for ok, copy in self.sent:
@@ -198,10 +211,11 @@
 
 def kernel(
     count, spins, points,
-    own, potential, row_factor, column_factor, left_high, left_low, green, wave,
-    updated, residual,
-    slots, table_high, table_low, density, other_density, cube, flat,
-    send_sem, recv_sem, swap_sem,
+    own_hbm, potential_hbm, row_hbm, column_hbm, left_high_hbm, left_low_hbm, green_hbm, wave_hbm,
+    negative,
+    slots, table_high, table_low, density, other_density, cube, flat, parts,
+    potential, row_factor, column_factor, left_high, left_low, green, wave,
+    send_sem, recv_sem, swap_sem, load_sem,
 ):
     volume = points**3
     plane = points * points
@@ -210,6 +224,20 @@
     me = lax.axis_index("band")
     spin = lax.axis_index("spin")
     relay = relayed(count, sizes)
+
+    own = slots.at[me]
+    loads = [
+        pltpu.make_async_copy(source, target, load_sem.at[k])
+        for k, (source, target) in enumerate(
+            (
+                (own_hbm, own), (row_hbm, row_factor), (column_hbm, column_factor),
+                (left_high_hbm, left_high), (left_low_hbm, left_low), (green_hbm, green),
+                (wave_hbm, wave), (potential_hbm, potential),
+            )
+        )
+    ]
+    for load in loads:
+        load.start()
 
     barrier = pltpu.get_barrier_semaphore()
     expected = jnp.int32(0)
@@ -235,8 +263,11 @@
         pl.semaphore_signal(
             barrier, inc=1, device_id=(lax.rem(spin + away, spins), me), device_id_type=MESH
         )
+    loads[0].wait()
     pl.semaphore_wait(barrier, expected + (spins - 1))
     gather.send_own()
+    for load in loads[1:]:
+        load.wait()
 
     def build(y, carry):
         rows = pl.ds(pl.multiple_of(y * points, points), points)
@@ -266,23 +297,30 @@
             [fields[k * points : (k + 1) * points] * f for k, f in enumerate(factors)], axis=0
         )
 
+    if relay:
+        onward, ending = gather.events()
+        for half, offsets in onward:
+            gather.take(half, offsets)
+
     resident = as_cube(own)
-    slots[me] = own[...]
     first = transform(jnp.concatenate([resident, resident * resident], axis=0))
     first = transform(scaled(first, (wave[...], green[...])))
     cube[...] = first[:points] - mixing * (first[points:] * resident)
 
     if relay:
-        for _, half, offsets in gather.events():
+        for half, offsets in ending:
             gather.take(half, offsets)
     else:
         gather.take_all()
+    unroll = count if count <= 16 else 1
 
     def add_square(j, total):
         band = slots[j]
         return total + band * band
 
-    density[...] = lax.fori_loop(0, count, add_square, jnp.zeros(own.shape, jnp.float32))
+    density[...] = lax.fori_loop(
+        0, count, add_square, jnp.zeros(density.shape, jnp.float32), unroll=unroll
+    )
     swaps = []
     for away in range(1, spins):
         swap = pltpu.make_async_remote_copy(
@@ -315,17 +353,18 @@
         flat[pl.ds(k, points, stride=blocks), :] = gradient[:, k * LANES : (k + 1) * LANES]
 
     def project(values):
-        def step(j, left):
-            band = slots[j]
-            share = jnp.sum(jnp.sum(band * values, axis=0, keepdims=True), axis=1, keepdims=True)
-            return left - (share / volume) * band
-
-        return lax.fori_loop(0, count, step, values)
-
-    flat[...] = project(flat[...])
-    result = project(flat[...])
-    residual[...] = result
-    updated[...] = own[...] - step_length * result
+        def overlap(j, carry):
+            parts[pl.ds(j, 1), :] = jnp.sum(slots[j] * values, axis=0, keepdims=True)
+            return carry
+
+        lax.fori_loop(0, count, overlap, 0, unroll=unroll)
+        shares = jnp.sum(parts[...], axis=1, keepdims=True) / volume
+        parts[...] = jnp.broadcast_to(shares, parts.shape)
+        return lax.fori_loop(
+            0, count, lambda j, left: left - parts[pl.ds(j, 1), :] * slots[j], values, unroll=unroll
+        )
+
+    negative[...] = -project(project(flat[...]))
     gather.finish()
 
 
@@ -359,16 +398,15 @@
     left_low = (left - left_high.astype(np.float32)).astype(jnp.bfloat16)
     sizes = line_sizes(count)
     if relayed(count, sizes):
-        sends = 12 + 4 * 2 * math.prod(len(offsets_of(s)) for s in sizes)
+        sends = 12 * len(PARTS) + 4 * len(PARTS) * math.prod(len(offsets_of(s)) for s in sizes)
     else:
         sends = count
-    vmem = pl.BlockSpec(memory_space=pltpu.VMEM)
-    flat_shape = jax.ShapeDtypeStruct((rows, LANES), jnp.float32)
-    updated, residual = pl.pallas_call(
+    constants = (row_factor, column_factor, left_high, left_low, green, wave)
+    negative = pl.pallas_call(
         functools.partial(kernel, count, spins, points),
-        out_shape=(flat_shape, flat_shape),
-        in_specs=[vmem] * 8,
-        out_specs=(vmem, vmem),
+        out_shape=jax.ShapeDtypeStruct((rows, LANES), jnp.float32),
+        in_specs=[pl.BlockSpec(memory_space=pl.ANY)] * 8,
+        out_specs=pl.BlockSpec(memory_space=pltpu.VMEM),
         scratch_shapes=[
             pltpu.VMEM((count, rows, LANES), jnp.float32),
             pltpu.VMEM((points * points, points * points), jnp.bfloat16),
@@ -377,18 +415,24 @@
             pltpu.VMEM((max(spins - 1, 1), rows, LANES), jnp.float32),
             pltpu.VMEM((points, points * points), jnp.float32),
             pltpu.VMEM((rows, LANES), jnp.float32),
+            pltpu.VMEM((count, LANES), jnp.float32),
+            pltpu.VMEM((rows, LANES), jnp.float32),
+        ]
+        + [pltpu.VMEM(c.shape, c.dtype) for c in constants]
+        + [
             pltpu.SemaphoreType.DMA((sends,)),
-            pltpu.SemaphoreType.DMA((2, count)),
+            pltpu.SemaphoreType.DMA((len(PARTS), count)),
             pltpu.SemaphoreType.DMA((2, max(spins - 1, 1))),
+            pltpu.SemaphoreType.DMA((8,)),
         ],
         compiler_params=pltpu.CompilerParams(
-            collective_id=0, has_side_effects=True, vmem_limit_bytes=60 * 1024 * 1024
+            collective_id=0,
+            has_side_effects=True,
+            vmem_limit_bytes=60 * 1024 * 1024,
         ),
-    )(
-        orbitals.reshape(rows, LANES), potential.reshape(rows, LANES),
-        row_factor, column_factor, left_high, left_low, green, wave,
-    )
-    return updated.reshape(orbitals.shape), residual.reshape(orbitals.shape)
+    )(orbitals.reshape(rows, LANES), potential.reshape(rows, LANES), *constants)
+    updated = orbitals.reshape(rows, LANES) + step_length * negative
+    return updated.reshape(orbitals.shape), (-negative).reshape(orbitals.shape)
 
 
 def solution(mesh):

time: 41.5 us -> 36.6 us (0.88)
  Pallas kernels: 38.4 us -> 34.1 us
  local copies, waits for them, and re-layouts: 2.26 us -> 0.01 us
  other arithmetic: 0 us -> 1.63 us
    pallas_call x1, Pallas kernels: 38.4 us -> 34.1 us  [per_device(): pl.pallas_call(functools.partial(kernel, count, spins, points), out_shape...]
    unnamed x4 -> x2, local copies, waits for them, and re-layouts: 2.26 us -> 0.01 us
    neg x0 -> x1, other arithmetic: none -> 1.63 us  [per_device(): -negative]
where the time goes in v2:
time: 36.6 us; the launch traced here: 36.4 us
  Pallas kernels  34.1 us (93%)
  other arithmetic  1.63 us (4%)
  between operations  0.65 us (2%)
    pallas_call x1, Pallas kernels, per_device(): pl.pallas_call(functools.partial(kernel, count, spins, points), out_shape...  34.1 us
    neg x1, other arithmetic, per_device(): -negative  1.63 us

profile of v2, /device:TPU:0, one launch (start us, length us, event | category | flops | bytes accessed | tf_op | source)
XLA Modules:
  0.0 36.4 jit_solution(2824830659488371323)
XLA Ops:
  0.6 0.0 copy-start
  0.6 34.1 %shard_map.95 = f32[256,128]{1,0:T(8,128)} custom-call(f32[256,128]{1,0:T(8,128)} %bitcast.4, f32[256,128]{1,0:T(8,128)} %bitcast.6, f32[32,1024]{1,0:T(8,128)} %constant.14.clone.row_hbm, f32[32,1024]{1,0:T(8,128)} %constant.15.clone.column_hbm, bf16[128,128]{1,0:T(8,128)(2,1)} %constant.16.clone.left_high_hbm, ...), custom_call_target="tpu_custom_call" | custom-call | tf_op jit(solution)/shard_map/pallas_call | solution.py:405
  34.8 0.0 copy-done
  34.8 1.6 %fusion = (f32[256,128]{1,0:T(8,128)}, f32[256,128]{1,0:T(8,128)}) fusion(f32[256,128]{1,0:T(8,128)} %shard_map.95, f32[256,128]{1,0:T(8,128)S(1)} %bitcast.5), kind=kLoop, calls=%fused_computation.1 | loop fusion | flops 98304 | bytes 524288 | tf_op jit(solution)/shard_map/neg | solution.py:435
Async XLA Ops:
  0.6 34.1 %copy-start = (f32[1,1,32768]{2,1,0:T(1,128)S(1)}, f32[1,1,32768]{2,1,0:T(1,128)}, u32[]{:S(2)}) copy-start(f32[1,1,32768]{2,1,0:T(1,128)} %param.8) | copy-start | bytes 393220

commit v3 on v2

--- a/solution.py
+++ b/solution.py
@@ -118,7 +118,7 @@
                     for x in offsets_of(self.sizes[2]):
                         if (z, y, x) != (0, 0, 0):
                             found.append((abs(z) + abs(y) + abs(x), half, (z, y, x)))
-        found = sorted(found, key=lambda e: (e[0], -e[1], -abs(e[2][0])))
+        found = sorted(found, key=lambda e: (e[2][1] + e[2][2], abs(e[2][0]), -e[1]))
         onward = [e[1:] for e in found if not self.ends(*e[1:])]
         return onward, [e[1:] for e in found if self.ends(*e[1:])]
 
@@ -335,18 +335,17 @@
         swaps.append(swap)
 
     partners = [as_cube(slots.at[lax.rem(me + o + count, count)]) for o in (1, 2, -1, -2)]
-    fields = transform(jnp.concatenate([resident * p for p in partners], axis=0))
-    fields = transform(scaled(fields, (green[...],) * len(partners)))
-    exchange = cube[...]
-    for k, p in enumerate(partners):
-        exchange = exchange - mixing * (fields[k * points : (k + 1) * points] * p)
-
     for swap in swaps:
         swap.wait()
     total = as_cube(density)
     for away in range(1, spins):
         total = total + as_cube(other_density.at[away - 1])
-    screened = transform(transform(total) * green[...])
+    fields = transform(jnp.concatenate([resident * p for p in partners] + [total], axis=0))
+    fields = transform(scaled(fields, (green[...],) * (len(partners) + 1)))
+    exchange = cube[...]
+    for k, p in enumerate(partners):
+        exchange = exchange - mixing * (fields[k * points : (k + 1) * points] * p)
+    screened = fields[len(partners) * points :]
     local = as_cube(potential) + hartree_weight * screened
     gradient = exchange + local * resident
     for k in range(blocks):
@@ -393,7 +392,7 @@
     volume = orbitals.shape[2]
     points = round(volume ** (1 / 3))
     rows = volume // LANES
-    row_factor, column_factor, left, green, wave = tables(points, 4)
+    row_factor, column_factor, left, green, wave = tables(points, 5)
     left_high = left.astype(jnp.bfloat16)
     left_low = (left - left_high.astype(np.float32)).astype(jnp.bfloat16)
     sizes = line_sizes(count)

time: 36.6 us -> 34.7 us (0.948)
  Pallas kernels: 34.1 us -> 32.2 us
    pallas_call x1, Pallas kernels: 34.1 us -> 32.2 us  [per_device(): pl.pallas_call(functools.partial(kernel, count, spins, points), out_shape...]
where the time goes in v3:
time: 34.7 us; the launch traced here: 34.5 us
  Pallas kernels  32.2 us (93%)
  other arithmetic  1.63 us (5%)
  between operations  0.65 us (2%)
    pallas_call x1, Pallas kernels, per_device(): pl.pallas_call(functools.partial(kernel, count, spins, points), out_shape...  32.2 us
    neg x1, other arithmetic, per_device(): -negative  1.63 us

profile of v3, /device:TPU:0, one launch (start us, length us, event | category | flops | bytes accessed | tf_op | source)
XLA Modules:
  0.0 34.5 jit_solution(15955925600682550476)
XLA Ops:
  0.6 0.0 copy-start
  0.6 32.2 %shard_map.95 = f32[256,128]{1,0:T(8,128)} custom-call(f32[256,128]{1,0:T(8,128)} %bitcast.4, f32[256,128]{1,0:T(8,128)} %bitcast.6, f32[32,1024]{1,0:T(8,128)} %constant.14.clone.row_hbm, f32[32,1024]{1,0:T(8,128)} %constant.15.clone.column_hbm, bf16[160,160]{1,0:T(8,128)(2,1)} %constant.16.clone.left_high_hbm, ...), custom_call_target="tpu_custom_call" | custom-call | tf_op jit(solution)/shard_map/pallas_call | solution.py:404
  32.9 0.0 copy-done
  32.9 1.6 %fusion = (f32[256,128]{1,0:T(8,128)}, f32[256,128]{1,0:T(8,128)}) fusion(f32[256,128]{1,0:T(8,128)} %shard_map.95, f32[256,128]{1,0:T(8,128)S(1)} %bitcast.5), kind=kLoop, calls=%fused_computation.1 | loop fusion | flops 98304 | bytes 524288 | tf_op jit(solution)/shard_map/neg | solution.py:434
Async XLA Ops:
  0.6 32.3 %copy-start = (f32[1,1,32768]{2,1,0:T(1,128)S(1)}, f32[1,1,32768]{2,1,0:T(1,128)}, u32[]{:S(2)}) copy-start(f32[1,1,32768]{2,1,0:T(1,128)} %param.8) | copy-start | bytes 393220
